TPU v7x, 256 devices: a whole 4x4x8 slice. The times are simulated.
256 devices in a mesh: replica: 64 (over x, z, core), shard: 4 (over y).
Axes of the slice: x: 4, y: 4, z: 8, core: 2. Of those that a mesh axis runs over, the one named last changes fastest.
Arguments:
- activations: bfloat16 [65536, 1536], P('replica'), may hold values from -6 to 6
- output_grads: bfloat16 [65536, 4, 1536], P('replica', None, 'shard'), may hold values from -0.00390625 to 0.00390625
- owner: int32 [4], replicated, may hold values from 0 to 3, each once
- step_count: int32 [1], replicated, may hold values from 1 to 40
- statistics: float32 [6144, 2, 1536], P(('replica', 'shard')), may hold values from -6 to 6
- inverse_roots: bfloat16 [6144, 2, 1536], P(('replica', 'shard')), may hold values from -1 to 2, as said below
- first_moment: float32 [6144, 1536], P(('replica', 'shard')), may hold values from -0.6 to 0.6
- second_moment: float32 [6144, 1536], P(('replica', 'shard')), may hold values from 0.005 to 0.05
Outputs:
- new_statistics: float32 [6144, 2, 1536], P(('replica', 'shard'))
- new_first: float32 [6144, 1536], P(('replica', 'shard'))
- new_second: float32 [6144, 1536], P(('replica', 'shard'))
- update: bfloat16 [4, 1536, 1536], P(None, None, 'shard')
Inputs may be any that keep to these rules, and one draw needn't show every extreme that they name: A permutation: block b belongs to the group of replicas b' * (16) to (b' + 1) * 16 - 1 with b' = owner[b]. `inverse_roots`: each matrix has positive diagonal entries.
All inputs are finite; a program needn't handle non-finite values.
Results may differ from a plain program's by a relative error of at most 0.0049.
Values may be sent and summed in bfloat16 or wider, within the bound.
No kernel may reach another device: no remote copies, remote signals or barrier semaphores. Data moves between devices by JAX's collectives and lax.ppermute only.
A program may use at most 128 MiB of HBM per device.

v0:
```python
import functools
import math
import jax
import jax.numpy as jnp
from jax import lax
from jax.sharding import Mesh
from jax.sharding import PartitionSpec as P

REPLICA = ("replica_0", "replica_1", "replica_2")
REPLICA_SHARD = ("replica_0", "replica_1", "replica_2", "shard")
beta_stat = 0.9
beta_first = 0.9
beta_second = 0.999
eps_adam = 1e-08
eps_norm = 1e-06


def in_order(pieces, dim):
    shape = list(pieces.shape[1:])
    shape[dim] *= pieces.shape[0]
    return jnp.moveaxis(pieces, 0, dim).reshape(shape)


def copy_for_each(value, axis):
    copies = jnp.broadcast_to(value, (lax.axis_size(axis), *value.shape))
    return lax.all_to_all(copies, axis, split_axis=0, concat_axis=0, tiled=True)


def gather_directly(value, axis, dim):
    return in_order(copy_for_each(value, axis), dim)


def partner_2(value, axis, apart):
    return lax.ppermute(value, axis, [(i, i ^ 1 << apart) for i in range(lax.axis_size(axis))])


def reduced_to_own(pieces, axes, order):
    shape = [lax.axis_size(a) for a in axes]
    pieces = pieces.reshape(*shape, *pieces.shape[1:])
    pieces = pieces.transpose(*order, *range(len(axes), pieces.ndim))
    pieces = pieces.reshape(-1, *pieces.shape[len(axes) :])
    for k in order:
        pieces = lax.psum_scatter(pieces, axes[k], scatter_dimension=0, tiled=True)
    return pieces[0]


def cut_along(value, dim, length):
    before, after = (value.shape[:dim], value.shape[dim + 1 :])
    return jnp.moveaxis(value.reshape(*before, length, -1, *after), dim, 0)


def scatter_axes(value, axes, order, dim):
    length = lax.axis_size(axes)
    return reduced_to_own(cut_along(value, dim, length), axes, order)


def one_axis_at_a_time(value, axes):
    return functools.reduce(lax.psum, axes, value)


def butterfly(values, concat_axis, group_bits, swap_values):
    position = lax.axis_index(REPLICA)
    for bit_number in range(group_bits):
        partner = swap_values(values, bit_number)
        upper = position >> bit_number & 1 == 1
        values = jnp.where(
            upper,
            jnp.concatenate([partner, values], concat_axis),
            jnp.concatenate([values, partner], concat_axis),
        )
    return values


def body(
    activations,
    output_grads,
    owner,
    step_count,
    statistics,
    inverse_roots,
    first_moment,
    second_moment,
):
    model_width = activations.shape[1]
    blocks_count = output_grads.shape[1]
    replicas = lax.axis_size(REPLICA)
    shards = lax.axis_size("shard")
    group_size = replicas // blocks_count
    group_bits = group_size.bit_length() - 1
    rows_dev = blocks_count * model_width // replicas
    span_rows = statistics.shape[0]
    owner_slot = lax.axis_index(REPLICA) // group_size
    local_index = lax.axis_index(REPLICA) % group_size
    span_index = local_index * shards + lax.axis_index("shard")
    root_rows = gather_directly(inverse_roots[:, 1, :], "shard", 0)
    whole_root = butterfly(
        root_rows, 0, group_bits, lambda values, bit_number: partner_2(values, REPLICA, bit_number)
    )
    slot_ids = jnp.arange(blocks_count, dtype=jnp.int32)
    onehot = (owner[None, :] == slot_ids[:, None]).astype(jnp.int32)
    source = jnp.sum(onehot * slot_ids[None, :], axis=1)
    grads_slot = jnp.take(output_grads, source, axis=1)
    piece_rows = math.gcd(rows_dev * lax.axis_size(REPLICA), model_width)

    def piece_product(piece_number):
        first_row = piece_number * piece_rows
        block_slot = first_row // model_width
        douts = lax.dynamic_index_in_dim(grads_slot, block_slot, 1, keepdims=False)
        return lax.dot_general(
            activations, douts, (((0,), (0,)), ((), ())), preferred_element_type=jnp.float32
        )

    pieces = lax.map(
        piece_product, jnp.arange(rows_dev * lax.axis_size(REPLICA) // piece_rows, dtype=jnp.int32)
    )
    reduced = scatter_axes(
        pieces.reshape(rows_dev * lax.axis_size(REPLICA), pieces.shape[-1]), REPLICA, (2, 0, 1), 0
    )
    exact_rows = lax.all_to_all(
        reduced.astype(jnp.bfloat16), "shard", split_axis=0, concat_axis=1, tiled=True
    ).astype(reduced.dtype)
    rounded = exact_rows.astype(jnp.bfloat16)
    block_rows = gather_directly(rounded, "shard", 0)
    full_grad = butterfly(
        block_rows, 0, group_bits, lambda values, bit_number: partner_2(values, REPLICA, bit_number)
    )
    grad_columns = lax.dynamic_slice_in_dim(full_grad, span_index * span_rows, span_rows, 1)
    left_gram = lax.dot_general(
        rounded, full_grad, (((1,), (1,)), ((), ())), preferred_element_type=jnp.float32
    )
    right_gram = lax.dot_general(
        grad_columns, full_grad, (((0,), (0,)), ((), ())), preferred_element_type=jnp.float32
    )
    new_left = beta_stat * statistics[:, 0, :] + (1.0 - beta_stat) * left_gram
    new_right = beta_stat * statistics[:, 1, :] + (1.0 - beta_stat) * right_gram
    count_float = step_count[0].astype(jnp.float32)
    first_new = beta_first * first_moment + (1.0 - beta_first) * exact_rows
    second_new = beta_second * second_moment + (1.0 - beta_second) * exact_rows * exact_rows
    first_hat = first_new / (1.0 - jnp.power(beta_first, count_float))
    second_hat = second_new / (1.0 - jnp.power(beta_second, count_float))
    adam_dir = first_hat / (jnp.sqrt(second_hat) + eps_adam)
    left_root = inverse_roots[:, 0, :]
    left_part = jnp.dot(left_root, full_grad, preferred_element_type=jnp.float32)
    precond = lax.dot_general(
        left_part,
        whole_root.astype(jnp.float32),
        (((1,), (1,)), ((), ())),
        precision=lax.Precision.HIGHEST,
    )
    slot_mask = (slot_ids == owner_slot).astype(jnp.float32)
    adam_total, precond_total = (
        one_axis_at_a_time(slot_mask * jnp.sum(adam_dir * adam_dir), REPLICA_SHARD),
        one_axis_at_a_time(slot_mask * jnp.sum(precond * precond), REPLICA_SHARD),
    )
    adam_squares = jnp.sum(adam_total * slot_mask)
    precond_squares = jnp.sum(precond_total * slot_mask)
    scale = jnp.sqrt(adam_squares) / (jnp.sqrt(precond_squares) + eps_norm)
    grafted = (precond * scale).astype(jnp.bfloat16)
    feature_rows = lax.all_to_all(grafted, "shard", split_axis=1, concat_axis=0, tiled=True)
    every_block = lax.all_gather(feature_rows, REPLICA, axis=0, tiled=True)
    update = jnp.take(
        every_block.reshape(blocks_count, model_width, every_block.shape[-1]), owner, axis=0
    )
    new_stats = jnp.stack([new_left, new_right], axis=1)
    return (new_stats, first_new, second_new, update)


def solution(mesh):
    torus = Mesh(
        mesh.devices.reshape(4, 8, 2, mesh.shape["shard"]),
        ("replica_0", "replica_1", "replica_2", "shard"),
    )
    placed = (
        P(REPLICA, None),
        P(REPLICA, None, "shard"),
        P(),
        P(),
        P(REPLICA_SHARD, None, None),
        P(REPLICA_SHARD, None, None),
        P(REPLICA_SHARD, None),
        P(REPLICA_SHARD, None),
    )
    return jax.shard_map(
        body,
        mesh=torus,
        in_specs=placed,
        out_specs=(
            P(REPLICA_SHARD, None, None),
            P(REPLICA_SHARD, None),
            P(REPLICA_SHARD, None),
            P(None, None, "shard"),
        ),
        check_vma=False,
    )
```

profile of v0, /device:TPU:1, one launch (start us, length us, event | category | flops | bytes accessed | tf_op | source)
XLA Modules:
  0.0 700.0 jit_solution(6775838303506029115)
XLA Ops:
  9.1 16.4 %gather_fusion = bf16[4,1024,384]{2,0,1:T(4,128)(2,1)} fusion(bf16[1024,4,384]{2,1,0:T(4,128)(2,1)S(1)} %copy-done, s32[1024]{0:T(1024)S(1)} %pad_clamp_fusion.1), kind=kCustom, calls=%fused_computation | custom fusion | bytes 6291472 | tf_op jit(solution)/shard_map/jit(_take)/gather | solution.py:102
  30.9 39.4 %while.12 = (s32[]{:T(128)}, f32[4,1536,384]{2,1,0:T(8,128)}, s32[4]{0:T(128)S(1)}, bf16[1024,4,384]{2,0,1:T(8,128)(2,1)}, bf16[1024,1536]{1,0:T(8,128)(2,1)}, /...) while((s32[]{:T(128)}, f32[4,1536,384]{2,1,0:T(8,128)}, ...), condition=%wide.region_2.3_spmd, body=%wide.region_1.2_spmd.sunk | while | flops 1207959552 | bytes 15728909 | solution.py:113
  51.9 5.0 convolution_bitcast_fusion.2
  70.3 8.1 %copy.28 = f32[2,4,8,96,384]{4,3,2,1,0:T(8,128)} copy(f32[2,4,8,96,384]{4,3,0,2,1:T(8,128)} %bitcast.70) | data formatting | bytes 18874368 | tf_op jit(solution)/shard_map/transpose | solution.py:40
  78.5 27.6 %reduce-scatter.4.cloned.1.call-done = f32[32,96,384]{2,1,0:T(8,128)} async-done(((f32[64,96,384]{2,1,0:T(8,128)}), f32[32,96,384]{2,1,0:T(8,128)}) %reduce-scatter.4.cloned.1.call-update) | async-done | bytes 4718608 | tf_op jit(solution)/shard_map/reduce_scatter | solution.py:43
  106.1 57.0 %reduce-scatter.6.cloned.1.call-done = f32[8,96,384]{2,1,0:T(8,128)} async-done(((f32[32,96,384]{2,1,0:T(8,128)}), f32[8,96,384]{2,1,0:T(8,128)}) %reduce-scatter.6.cloned.1.call-update) | async-done | bytes 1179664 | tf_op jit(solution)/shard_map/reduce_scatter | solution.py:43
  163.2 36.9 %reduce-scatter.8.cloned.1.call-done = f32[1,96,384]{2,1,0:T(8,128)} async-done(((f32[8,96,384]{2,1,0:T(8,128)}), f32[1,96,384]{2,1,0:T(8,128)}) %reduce-scatter.8.cloned.1.call-update) | async-done | bytes 147472 | tf_op jit(solution)/shard_map/reduce_scatter | solution.py:43
  201.0 8.1 %all_to_all.45 = bf16[4,24,384]{2,1,0:T(8,128)(2,1)S(1)} all-to-all(bf16[4,24,384]{2,1,0:T(8,128)(2,1)S(1)} %bitcast.80), channel_id=1, replica_groups=mesh['replica_0'=4,'replica_1'=8,'replica_2'=2,'shard'=4] {'shard'}, dimensions={0} | all-to-all | bytes 147456 | tf_op jit(solution)/shard_map/all_to_all | solution.py:119
  209.2 8.1 %all_to_all.46 = bf16[4,24,1536]{2,1,0:T(8,128)(2,1)S(1)} all-to-all(bf16[4,24,1536]{2,1,0:T(8,128)(2,1)S(1)} %broadcast_in_dim.44), channel_id=1, replica_groups=mesh['replica_0'=4,'replica_1'=8,'replica_2'=2,'shard'=4] {'shard'}, dimensions={0} | all-to-all | bytes 589824 | tf_op jit(solution)/shard_map/all_to_all | solution.py:26
  217.2 7.8 %collective-permute-start = (bf16[96,1536]{1,0:T(8,128)(2,1)S(1)}, bf16[96,1536]{1,0:T(8,128)(2,1)S(1)}, u32[]{:S(2)}, u32[]{:S(2)}) collective-permute-start(bf16[96,1536]{1,0:T(8,128)(2,1)S(1)} %bitcast.72), channel_id=1, source_target_pairs={{0,4},{4,0},{8,12},{12,8},{16,20},{20,16},{24,28},{28,24},{32,36},... | collective-permute-start | bytes 884744 | tf_op jit(solution)/shard_map/ppermute | solution.py:34
  231.6 6.1 all-to-all-done.2
  244.8 35.8 %collective-permute-done.5 = bf16[192,1536]{1,0:T(8,128)(2,1)S(1)} collective-permute-done((bf16[192,1536]{1,0:T(8,128)(2,1)S(1)}, bf16[192,1536]{1,0:T(8,128)(2,1)S(1)}, u32[]{:S(2)}, u32[]{:S(2)}) %collective-permute-start.5) | collective-permute-done | bytes 589856 | tf_op jit(solution)/shard_map/ppermute | solution.py:34
  282.9 37.5 %collective-permute-done.2 = bf16[384,1536]{1,0:T(8,128)(2,1)} collective-permute-done((bf16[384,1536]{1,0:T(8,128)(2,1)S(1)}, bf16[384,1536]{1,0:T(8,128)(2,1)}, u32[]{:S(2)}, u32[]{:S(2)}) %collective-permute-start.2) | collective-permute-done | bytes 1179680 | tf_op jit(solution)/shard_map/ppermute | solution.py:34
  325.6 71.3 %collective-permute-done.6 = bf16[384,1536]{1,0:T(8,128)(2,1)S(1)} collective-permute-done((bf16[384,1536]{1,0:T(8,128)(2,1)S(1)}, bf16[384,1536]{1,0:T(8,128)(2,1)S(1)}, u32[]{:S(2)}, u32[]{:S(2)}) %collective-permute-start.6) | collective-permute-done | bytes 1179680 | tf_op jit(solution)/shard_map/ppermute | solution.py:34
  410.7 142.4 %collective-permute-done.7 = bf16[768,1536]{1,0:T(8,128)(2,1)} collective-permute-done((bf16[768,1536]{1,0:T(8,128)(2,1)}, bf16[768,1536]{1,0:T(8,128)(2,1)}, u32[]{:S(2)}, u32[]{:S(2)}) %collective-permute-start.7) | collective-permute-done | bytes 2359328 | tf_op jit(solution)/shard_map/ppermute | solution.py:34
  553.1 7.1 %multiply_reduce_fusion = (f32[]{:T(128)}, f32[24,1536]{1,0:T(8,128)S(1)}) fusion(f32[1536,24]{0,1:T(8,128)S(1)} %fusion.19, bf16[768,1536]{1,0:T(8,128)(2,1)} %maximum_select_fusion.4, bf16[768,1536]{1,0:T(8,128)(2,1)} %collective-permute-done.7, pred[]{:T(512)S(6)} %eq.40), kind=kOutput, calls=%fused_computation.41 | convolution fusion | flops 700784640 | bytes 5013509 | tf_op jit(solution)/shard_map/dot_general | solution.py:144
  560.8 8.3 %all-reduce.2 = (f32[4]{0:T(128)S(1)}, f32[4]{0:T(128)S(1)}) all-reduce(f32[4]{0:T(128)S(1)} %fusion.22, f32[4]{0:T(128)S(1)} %fusion.21), channel_id=1, replica_groups=mesh['replica_0'=4,'replica_1'=8,'replica_2'=2,'shard'=4] {'replica_0'}, use_global_device_ids=true, to_apply=%region_7.8 | all-reduce | flops 8 | bytes 64 | tf_op jit(solution)/shard_map/psum | solution.py:58
  569.1 11.1 %all-reduce = (f32[4]{0:T(128)S(1)}, f32[4]{0:T(128)S(1)}) all-reduce(f32[4]{0:T(128)S(1)} %get-tuple-element.107, f32[4]{0:T(128)S(1)} %get-tuple-element.108), channel_id=1, replica_groups=mesh['replica_0'=4,'replica_1'=8,'replica_2'=2,'shard'=4] {'replica_1'}, use_global_device_ids=true, to_apply=%region_8.9 | all-reduce | flops 8 | bytes 64 | tf_op jit(solution)/shard_map/psum | solution.py:58
  580.2 8.4 %all-reduce.3 = (f32[4]{0:T(128)S(1)}, f32[4]{0:T(128)S(1)}) all-reduce(f32[4]{0:T(128)S(1)} %get-tuple-element.103, f32[4]{0:T(128)S(1)} %get-tuple-element.104), channel_id=1, replica_groups=mesh['replica_0'=4,'replica_1'=8,'replica_2'=2,'shard'=4] {'replica_2'}, use_global_device_ids=true, to_apply=%region_9.10 | all-reduce | flops 8 | bytes 64 | tf_op jit(solution)/shard_map/psum | solution.py:58
  588.6 6.8 all-reduce.1
  597.6 7.6 %all_to_all.47 = bf16[24,4,384]{2,0,1:T(8,128)(2,1)} all-to-all(bf16[24,4,384]{2,0,1:T(8,128)(2,1)S(1)} %bitcast.84), channel_id=1, replica_groups=mesh['replica_0'=4,'replica_1'=8,'replica_2'=2,'shard'=4] {'shard'}, dimensions={1} | all-to-all | bytes 147456 | tf_op jit(solution)/shard_map/all_to_all | solution.py:159
  611.5 70.9 %all-gather.2.cloned.1.call-done = bf16[6144,384]{1,0:T(8,128)(2,1)} async-done(((bf16[96,384]{1,0:T(8,128)(2,1)}), bf16[6144,384]{1,0:T(8,128)(2,1)}) %all-gather.2.cloned.1.call-update) | async-done | bytes 4718608 | tf_op jit(solution)/shard_map/all_gather | solution.py:160
  682.4 5.9 gather_fusion.1
  688.3 5.1 broadcast_select_fusion
  (91 shorter events, 81.8 us)
Async XLA Ops:
  7.2 1.9 copy-start
  7.2 98.9 %reduce-scatter.4.cloned.1.call-start = ((), (), s32[]{:S(2)}) async-start(), calls=%async_computation.7 | async-start | bytes 14155776 | tf_op jit(solution)/shard_map/reduce_scatter | solution.py:43
  78.4 84.7 %reduce-scatter.6.cloned.1.call-start = ((), (), s32[]{:S(2)}) async-start(), calls=%async_computation.8 | async-start | bytes 5898240 | tf_op jit(solution)/shard_map/reduce_scatter | solution.py:43
  106.0 121.1 %copy-start.5 = (bf16[24,2,1536]{2,1,0:T(2,128)(2,1)S(1)}, bf16[24,2,1536]{2,1,0:T(2,128)(2,1)}, u32[]{:S(2)}) copy-start(bf16[24,2,1536]{2,1,0:T(2,128)(2,1)} %param.15) | copy-start | bytes 442372
  106.1 94.0 %reduce-scatter.8.cloned.1.call-start = ((), (), s32[]{:S(2)}) async-start(), calls=%async_computation.9 | async-start | bytes 1327104 | tf_op jit(solution)/shard_map/reduce_scatter | solution.py:43
  217.2 9.0 %collective-permute-start = (bf16[96,1536]{1,0:T(8,128)(2,1)S(1)}, bf16[96,1536]{1,0:T(8,128)(2,1)S(1)}, u32[]{:S(2)}, u32[]{:S(2)}) collective-permute-start(bf16[96,1536]{1,0:T(8,128)(2,1)S(1)} %bitcast.72), channel_id=1, source_target_pairs={{0,4},{4,0},{8,12},{12,8},{16,20},{20,16},{24,28},{28,24},{32,36},... | collective-permute-start | bytes 884744 | tf_op jit(solution)/shard_map/ppermute | solution.py:34
  226.3 14.6 %collective-permute-start.1 = (bf16[192,1536]{1,0:T(8,128)(2,1)S(1)}, bf16[192,1536]{1,0:T(8,128)(2,1)S(1)}, u32[]{:S(2)}, u32[]{:S(2)}) collective-permute-start(bf16[192,1536]{1,0:T(8,128)(2,1)S(1)} %maximum_select_fusion.7), channel_id=1, source_target_pairs={{0,8},{4,12},{8,0},{12,4},{16,24},{20,28},{24,16},{28,20},{32,40},... | collective-permute-start | bytes 1769480 | tf_op jit(solution)/shard_map/ppermute | solution.py:34
  228.1 9.6 %all-to-all-start.2 = ((bf16[4,24,1536]{2,1,0:T(8,128)(2,1)}), bf16[4,24,1536]{2,1,0:T(8,128)(2,1)S(1)}, u32[]{:S(2)}, u32[]{:S(2)}) async-start(bf16[4,24,1536]{2,1,0:T(8,128)(2,1)} %broadcast_in_dim.46), calls=%async_computation.5 | async-start | bytes 589824 | tf_op jit(solution)/shard_map/all_to_all | solution.py:26
  231.5 450.9 %all-gather.2.cloned.1.call-start = ((), (), s32[]{:S(2)}) async-start(), calls=%async_computation.10 | async-start | bytes 4792320 | tf_op jit(solution)/shard_map/all_gather | solution.py:160
  237.7 5.8 collective-permute-start.4
  241.4 41.5 %copy-start.4 = (bf16[384,1536]{1,0:T(8,128)(2,1)}, bf16[384,1536]{1,0:T(8,128)(2,1)S(1)}, u32[]{:S(2)}) copy-start(bf16[384,1536]{1,0:T(8,128)(2,1)S(1)} %maximum_select_fusion.5) | copy-start | bytes 3538948
  241.4 79.0 %collective-permute-start.2 = (bf16[384,1536]{1,0:T(8,128)(2,1)S(1)}, bf16[384,1536]{1,0:T(8,128)(2,1)}, u32[]{:S(2)}, u32[]{:S(2)}) collective-permute-start(bf16[384,1536]{1,0:T(8,128)(2,1)S(1)} %maximum_select_fusion.5), channel_id=1, source_target_pairs={{0,16},{4,20},{8,24},{12,28},{16,0},{20,4},{24,8},{28,12},{32,48},... | collective-permute-start | bytes 3538952 | tf_op jit(solution)/shard_map/ppermute | solution.py:34
  243.6 37.0 %collective-permute-start.5 = (bf16[192,1536]{1,0:T(8,128)(2,1)S(1)}, bf16[192,1536]{1,0:T(8,128)(2,1)S(1)}, u32[]{:S(2)}, u32[]{:S(2)}) collective-permute-start(bf16[192,1536]{1,0:T(8,128)(2,1)S(1)} %maximum_select_fusion.8), channel_id=1, source_target_pairs={{0,8},{4,12},{8,0},{12,4},{16,24},{20,28},{24,16},{28,20},{32,40},... | collective-permute-start | bytes 1769480 | tf_op jit(solution)/shard_map/ppermute | solution.py:34
  280.9 115.9 %collective-permute-start.6 = (bf16[384,1536]{1,0:T(8,128)(2,1)S(1)}, bf16[384,1536]{1,0:T(8,128)(2,1)S(1)}, u32[]{:S(2)}, u32[]{:S(2)}) collective-permute-start(bf16[384,1536]{1,0:T(8,128)(2,1)S(1)} %maximum_select_fusion.6), channel_id=1, source_target_pairs={{0,16},{4,20},{8,24},{12,28},{16,0},{20,4},{24,8},{28,12},{32,48},... | collective-permute-start | bytes 3538952 | tf_op jit(solution)/shard_map/ppermute | solution.py:34
  323.1 78.6 %copy-start.7 = (f32[24,1536]{1,0:T(8,128)S(1)}, f32[24,1536]{1,0:T(8,128)}, u32[]{:S(2)}) copy-start(f32[24,1536]{1,0:T(8,128)} %param.17) | copy-start | bytes 442372
  323.1 78.6 %copy-start.8 = (f32[24,1536]{1,0:T(8,128)S(1)}, f32[24,1536]{1,0:T(8,128)}, u32[]{:S(2)}) copy-start(f32[24,1536]{1,0:T(8,128)} %param.16) | copy-start | bytes 442372
  323.1 80.8 %collective-permute-start.3 = (bf16[768,1536]{1,0:T(8,128)(2,1)S(1)}, bf16[768,1536]{1,0:T(8,128)(2,1)}, u32[]{:S(2)}, u32[]{:S(2)}) collective-permute-start(bf16[768,1536]{1,0:T(8,128)(2,1)S(1)} %maximum_select_fusion.3), channel_id=1, source_target_pairs={{0,32},{4,36},{8,40},{12,44},{16,48},{20,52},{24,56},{28,60},{32,0... | collective-permute-start | bytes 7077896 | tf_op jit(solution)/shard_map/ppermute | solution.py:34
  398.6 154.5 %collective-permute-start.7 = (bf16[768,1536]{1,0:T(8,128)(2,1)}, bf16[768,1536]{1,0:T(8,128)(2,1)}, u32[]{:S(2)}, u32[]{:S(2)}) collective-permute-start(bf16[768,1536]{1,0:T(8,128)(2,1)} %maximum_select_fusion.4), channel_id=1, source_target_pairs={{0,32},{4,36},{8,40},{12,44},{16,48},{20,52},{24,56},{28,60},{32,0... | collective-permute-start | bytes 7077896 | tf_op jit(solution)/shard_map/ppermute | solution.py:34
  407.8 2.2 copy-start.2
  410.7 194.5 %copy-start.9 = (s32[4]{0:T(128)S(1)}, s32[4]{0:T(128)}, u32[]{:S(2)}) copy-start(s32[4]{0:T(128)} %param.12) | copy-start | bytes 52
  410.7 194.5 %copy-start.6 = (f32[24,2,1536]{2,1,0:T(2,128)S(1)}, f32[24,2,1536]{2,1,0:T(2,128)}, u32[]{:S(2)}) copy-start(f32[24,2,1536]{2,1,0:T(2,128)} %param.14) | copy-start | bytes 884740
  605.2 4.0 copy-start.3
  682.4 11.0 %copy-start.1 = (bf16[1024,4,384]{2,1,0:T(4,128)(2,1)S(1)}, bf16[1024,4,384]{2,1,0:T(4,128)(2,1)}, u32[]{:S(2)}) copy-start(bf16[1024,4,384]{2,1,0:T(4,128)(2,1)} %param.11) | copy-start | bytes 9437188
Sparse Core Ops, SparseCore 0:
  78.5 27.4 reduce-scatter.3
  108.6 54.5 reduce-scatter.5
  165.7 34.3 reduce-scatter.7
  605.3 77.0 all-gather.1
where the time goes:
time: 701 us; the launch traced here: 700 us
  waiting for transfers between devices  488 us (70%)
  blocking collectives  58.3 us (8%)
  local copies, waits for them, and re-layouts  54.7 us (8%)
  matrix products  32.5 us (5%)
  starting transfers between devices  24 us (3%)
  other arithmetic  23.2 us (3%)
  between operations  16.3 us (2%)
    ppermute x8, waiting for transfers between devices, partner_2(): lax.ppermute(value, axis, [(i, i ^ 1 << apart) for i in range(lax.axis_si...  290 us
    reduce_scatter x3, waiting for transfers between devices, reduced_to_own(): pieces = lax.psum_scatter(pieces, axes[k], scatter_dimension=0, tiled=True)  122 us
    all_gather x1, waiting for transfers between devices, body(): every_block = lax.all_gather(feature_rows, REPLICA, axis=0, tiled=True)  70.9 us
    psum x4, blocking collectives, one_axis_at_a_time(): return functools.reduce(lax.psum, axes, value)  34.6 us
    ppermute x8, starting transfers between devices, partner_2(): lax.ppermute(value, axis, [(i, i ^ 1 << apart) for i in range(lax.axis_si...  20.4 us
    dot_general x4, matrix products, piece_product(): lax.dot_general(activations, douts, (((0,), (0,)), ((), ())), preferred_e...  19.8 us
    gather x1, local copies, waits for them, and re-layouts, body(): grads_slot = jnp.take(output_grads, source, axis=1)  16.4 us
    dynamic_update_slice x8, local copies, waits for them, and re-layouts, body(): lax.map(piece_product, jnp.arange(rows_dev * lax.axis_size(REPLICA) // pi...  14.5 us
  transfers between devices with their start and end apart: 13, of which 11 were waited for; matrix products, arithmetic and copies ran while one was open for 3% of the time, Pallas kernels for 0%

commit v1 on v0

--- a/solution.py
+++ b/solution.py
@@ -157,7 +157,9 @@
     scale = jnp.sqrt(adam_squares) / (jnp.sqrt(precond_squares) + eps_norm)
     grafted = (precond * scale).astype(jnp.bfloat16)
     feature_rows = lax.all_to_all(grafted, "shard", split_axis=1, concat_axis=0, tiled=True)
-    every_block = lax.all_gather(feature_rows, REPLICA, axis=0, tiled=True)
+    every_block = jnp.concatenate(
+        lax.all_to_all(jnp.stack([feature_rows] * lax.axis_size(REPLICA)), REPLICA, 0, 0), axis=0
+    )
     update = jnp.take(
         every_block.reshape(blocks_count, model_width, every_block.shape[-1]), owner, axis=0
     )

time: 701 us -> 742 us (1.058)
  waiting for transfers between devices: 488 us -> 517 us
  starting transfers between devices: 24 us -> 32.3 us
    all_to_all x0 -> x1, waiting for transfers between devices: none -> 98.8 us  [body(): lax.all_to_all(jnp.stack([feature_rows] * lax.axis_size(REPLICA)), REPLIC...]
    all_gather x1 -> x0, waiting for transfers between devices: 70.9 us -> none  [body(): every_block = lax.all_gather(feature_rows, REPLICA, axis=0, tiled=True)]
    all_to_all x0 -> x1, starting transfers between devices: none -> 8.74 us  [body(): lax.all_to_all(jnp.stack([feature_rows] * lax.axis_size(REPLICA)), REPLIC...]
where the time goes in v1:
time: 742 us; the launch traced here: 741 us
  waiting for transfers between devices  517 us (70%)
  blocking collectives  57.8 us (8%)
  local copies, waits for them, and re-layouts  57.1 us (8%)
  matrix products  34.9 us (5%)
  starting transfers between devices  32.3 us (4%)
  other arithmetic  22.9 us (3%)
  between operations  16.2 us (2%)
    ppermute x8, waiting for transfers between devices, partner_2(): lax.ppermute(value, axis, [(i, i ^ 1 << apart) for i in range(lax.axis_si...  290 us
    reduce_scatter x3, waiting for transfers between devices, reduced_to_own(): pieces = lax.psum_scatter(pieces, axes[k], scatter_dimension=0, tiled=True)  122 us
    all_to_all x1, waiting for transfers between devices, body(): lax.all_to_all(jnp.stack([feature_rows] * lax.axis_size(REPLICA)), REPLIC...  98.8 us
    psum x4, blocking collectives, one_axis_at_a_time(): return functools.reduce(lax.psum, axes, value)  34.6 us
    ppermute x8, starting transfers between devices, partner_2(): lax.ppermute(value, axis, [(i, i ^ 1 << apart) for i in range(lax.axis_si...  20 us
    dot_general x4, matrix products, piece_product(): lax.dot_general(activations, douts, (((0,), (0,)), ((), ())), preferred_e...  19.9 us
    gather x1, local copies, waits for them, and re-layouts, body(): grads_slot = jnp.take(output_grads, source, axis=1)  16.4 us
  transfers between devices with their start and end apart: 13, of which 11 were waited for; matrix products, arithmetic and copies ran while one was open for 3% of the time, Pallas kernels for 0%

profile of v1, /device:TPU:1, one launch (start us, length us, event | category | flops | bytes accessed | tf_op | source)
XLA Modules:
  0.0 740.6 jit_solution(17878925359848535890)
XLA Ops:
  9.1 16.4 %gather_fusion = bf16[4,1024,384]{2,0,1:T(4,128)(2,1)} fusion(bf16[1024,4,384]{2,1,0:T(4,128)(2,1)S(1)} %copy-done, s32[1024]{0:T(1024)S(1)} %pad_clamp_fusion.1), kind=kCustom, calls=%fused_computation | custom fusion | bytes 6291472 | tf_op jit(solution)/shard_map/jit(_take)/gather | solution.py:102
  30.9 39.4 %while.12 = (s32[]{:T(128)}, f32[4,1536,384]{2,1,0:T(8,128)}, s32[4]{0:T(128)S(1)}, bf16[1024,4,384]{2,0,1:T(8,128)(2,1)}, bf16[1024,1536]{1,0:T(8,128)(2,1)}, /...) while((s32[]{:T(128)}, f32[4,1536,384]{2,1,0:T(8,128)}, ...), condition=%wide.region_2.3_spmd, body=%wide.region_1.2_spmd.sunk | while | flops 1207959552 | bytes 15728909 | solution.py:113
  70.3 8.1 %copy.28 = f32[2,4,8,96,384]{4,3,2,1,0:T(8,128)} copy(f32[2,4,8,96,384]{4,3,0,2,1:T(8,128)} %bitcast.70) | data formatting | bytes 18874368 | tf_op jit(solution)/shard_map/transpose | solution.py:40
  78.5 27.6 %reduce-scatter.4.cloned.1.call-done = f32[32,96,384]{2,1,0:T(8,128)} async-done(((f32[64,96,384]{2,1,0:T(8,128)}), f32[32,96,384]{2,1,0:T(8,128)}) %reduce-scatter.4.cloned.1.call-update) | async-done | bytes 4718608 | tf_op jit(solution)/shard_map/reduce_scatter | solution.py:43
  106.2 57.0 %reduce-scatter.6.cloned.1.call-done = f32[8,96,384]{2,1,0:T(8,128)} async-done(((f32[32,96,384]{2,1,0:T(8,128)}), f32[8,96,384]{2,1,0:T(8,128)}) %reduce-scatter.6.cloned.1.call-update) | async-done | bytes 1179664 | tf_op jit(solution)/shard_map/reduce_scatter | solution.py:43
  163.2 37.1 %reduce-scatter.8.cloned.1.call-done = f32[1,96,384]{2,1,0:T(8,128)} async-done(((f32[8,96,384]{2,1,0:T(8,128)}), f32[1,96,384]{2,1,0:T(8,128)}) %reduce-scatter.8.cloned.1.call-update) | async-done | bytes 147472 | tf_op jit(solution)/shard_map/reduce_scatter | solution.py:43
  201.2 8.2 %all_to_all.47 = bf16[4,24,384]{2,1,0:T(8,128)(2,1)S(1)} all-to-all(bf16[4,24,384]{2,1,0:T(8,128)(2,1)S(1)} %bitcast.79), channel_id=1, replica_groups=mesh['replica_0'=4,'replica_1'=8,'replica_2'=2,'shard'=4] {'shard'}, dimensions={0} | all-to-all | bytes 147456 | tf_op jit(solution)/shard_map/all_to_all | solution.py:119
  209.5 8.1 %all_to_all.48 = bf16[4,24,1536]{2,1,0:T(8,128)(2,1)S(1)} all-to-all(bf16[4,24,1536]{2,1,0:T(8,128)(2,1)S(1)} %broadcast_in_dim.44), channel_id=1, replica_groups=mesh['replica_0'=4,'replica_1'=8,'replica_2'=2,'shard'=4] {'shard'}, dimensions={0} | all-to-all | bytes 589824 | tf_op jit(solution)/shard_map/all_to_all | solution.py:26
  217.5 7.5 %collective-permute-start = (bf16[96,1536]{1,0:T(8,128)(2,1)S(1)}, bf16[96,1536]{1,0:T(8,128)(2,1)S(1)}, u32[]{:S(2)}, u32[]{:S(2)}) collective-permute-start(bf16[96,1536]{1,0:T(8,128)(2,1)S(1)} %bitcast.71), channel_id=1, source_target_pairs={{0,4},{4,0},{8,12},{12,8},{16,20},{20,16},{24,28},{28,24},{32,36},... | collective-permute-start | bytes 884744 | tf_op jit(solution)/shard_map/ppermute | solution.py:34
  231.6 6.1 all-to-all-done.2
  244.8 35.8 %collective-permute-done.5 = bf16[192,1536]{1,0:T(8,128)(2,1)S(1)} collective-permute-done((bf16[192,1536]{1,0:T(8,128)(2,1)S(1)}, bf16[192,1536]{1,0:T(8,128)(2,1)S(1)}, u32[]{:S(2)}, u32[]{:S(2)}) %collective-permute-start.5) | collective-permute-done | bytes 589856 | tf_op jit(solution)/shard_map/ppermute | solution.py:34
  282.8 37.6 %collective-permute-done.2 = bf16[384,1536]{1,0:T(8,128)(2,1)} collective-permute-done((bf16[384,1536]{1,0:T(8,128)(2,1)S(1)}, bf16[384,1536]{1,0:T(8,128)(2,1)}, u32[]{:S(2)}, u32[]{:S(2)}) %collective-permute-start.2) | collective-permute-done | bytes 1179680 | tf_op jit(solution)/shard_map/ppermute | solution.py:34
  325.6 71.3 %collective-permute-done.6 = bf16[384,1536]{1,0:T(8,128)(2,1)S(1)} collective-permute-done((bf16[384,1536]{1,0:T(8,128)(2,1)S(1)}, bf16[384,1536]{1,0:T(8,128)(2,1)S(1)}, u32[]{:S(2)}, u32[]{:S(2)}) %collective-permute-start.6) | collective-permute-done | bytes 1179680 | tf_op jit(solution)/shard_map/ppermute | solution.py:34
  410.6 142.5 %collective-permute-done.7 = bf16[768,1536]{1,0:T(8,128)(2,1)} collective-permute-done((bf16[768,1536]{1,0:T(8,128)(2,1)}, bf16[768,1536]{1,0:T(8,128)(2,1)}, u32[]{:S(2)}, u32[]{:S(2)}) %collective-permute-start.7) | collective-permute-done | bytes 2359328 | tf_op jit(solution)/shard_map/ppermute | solution.py:34
  553.1 7.2 multiply_reduce_fusion
  561.0 8.4 %all-reduce.2 = (f32[4]{0:T(128)S(1)}, f32[4]{0:T(128)S(1)}) all-reduce(f32[4]{0:T(128)S(1)} %fusion.22, f32[4]{0:T(128)S(1)} %fusion.21), channel_id=1, replica_groups=mesh['replica_0'=4,'replica_1'=8,'replica_2'=2,'shard'=4] {'replica_0'}, use_global_device_ids=true, to_apply=%region_7.8 | all-reduce | flops 8 | bytes 64 | tf_op jit(solution)/shard_map/psum | solution.py:58
  569.4 11.0 %all-reduce = (f32[4]{0:T(128)S(1)}, f32[4]{0:T(128)S(1)}) all-reduce(f32[4]{0:T(128)S(1)} %get-tuple-element.107, f32[4]{0:T(128)S(1)} %get-tuple-element.108), channel_id=1, replica_groups=mesh['replica_0'=4,'replica_1'=8,'replica_2'=2,'shard'=4] {'replica_1'}, use_global_device_ids=true, to_apply=%region_8.9 | all-reduce | flops 8 | bytes 64 | tf_op jit(solution)/shard_map/psum | solution.py:58
  580.4 8.4 %all-reduce.3 = (f32[4]{0:T(128)S(1)}, f32[4]{0:T(128)S(1)}) all-reduce(f32[4]{0:T(128)S(1)} %get-tuple-element.103, f32[4]{0:T(128)S(1)} %get-tuple-element.104), channel_id=1, replica_groups=mesh['replica_0'=4,'replica_1'=8,'replica_2'=2,'shard'=4] {'replica_2'}, use_global_device_ids=true, to_apply=%region_9.10 | all-reduce | flops 8 | bytes 64 | tf_op jit(solution)/shard_map/psum | solution.py:58
  588.8 6.8 all-reduce.1
  597.7 6.9 all_to_all.49
  607.1 8.7 %all-to-all-start.4 = ((bf16[64,96,384]{2,1,0:T(8,128)(2,1)}), bf16[64,96,384]{2,1,0:T(8,128)(2,1)}, u32[]{:S(2)}, u32[]{:S(2)}) async-start(bf16[64,96,384]{2,1,0:T(8,128)(2,1)} %stack.14), calls=%async_computation.7 | async-start | bytes 9437184 | tf_op jit(solution)/shard_map/all_to_all | solution.py:161
  624.3 98.8 %all-to-all-done.4 = bf16[64,96,384]{2,1,0:T(8,128)(2,1)} async-done(((bf16[64,96,384]{2,1,0:T(8,128)(2,1)}), bf16[64,96,384]{2,1,0:T(8,128)(2,1)}, u32[]{:S(2)}, u32[]{:S(2)}) %all-to-all-start.4) | async-done | bytes 4718624 | tf_op jit(solution)/shard_map/all_to_all | solution.py:161
  723.1 5.9 gather_fusion.1
  728.9 5.1 broadcast_select_fusion
  (89 shorter events, 91.0 us)
Async XLA Ops:
  7.2 1.9 copy-start
  7.2 98.9 %reduce-scatter.4.cloned.1.call-start = ((), (), s32[]{:S(2)}) async-start(), calls=%async_computation.8 | async-start | bytes 14155776 | tf_op jit(solution)/shard_map/reduce_scatter | solution.py:43
  78.4 84.7 %reduce-scatter.6.cloned.1.call-start = ((), (), s32[]{:S(2)}) async-start(), calls=%async_computation.9 | async-start | bytes 5898240 | tf_op jit(solution)/shard_map/reduce_scatter | solution.py:43
  106.1 121.1 %copy-start.4 = (bf16[24,2,1536]{2,1,0:T(2,128)(2,1)S(1)}, bf16[24,2,1536]{2,1,0:T(2,128)(2,1)}, u32[]{:S(2)}) copy-start(bf16[24,2,1536]{2,1,0:T(2,128)(2,1)} %param.15) | copy-start | bytes 442372
  106.1 94.1 %reduce-scatter.8.cloned.1.call-start = ((), (), s32[]{:S(2)}) async-start(), calls=%async_computation.10 | async-start | bytes 1327104 | tf_op jit(solution)/shard_map/reduce_scatter | solution.py:43
  217.5 8.7 %collective-permute-start = (bf16[96,1536]{1,0:T(8,128)(2,1)S(1)}, bf16[96,1536]{1,0:T(8,128)(2,1)S(1)}, u32[]{:S(2)}, u32[]{:S(2)}) collective-permute-start(bf16[96,1536]{1,0:T(8,128)(2,1)S(1)} %bitcast.71), channel_id=1, source_target_pairs={{0,4},{4,0},{8,12},{12,8},{16,20},{20,16},{24,28},{28,24},{32,36},... | collective-permute-start | bytes 884744 | tf_op jit(solution)/shard_map/ppermute | solution.py:34
  226.4 14.6 %collective-permute-start.1 = (bf16[192,1536]{1,0:T(8,128)(2,1)S(1)}, bf16[192,1536]{1,0:T(8,128)(2,1)S(1)}, u32[]{:S(2)}, u32[]{:S(2)}) collective-permute-start(bf16[192,1536]{1,0:T(8,128)(2,1)S(1)} %maximum_select_fusion.7), channel_id=1, source_target_pairs={{0,8},{4,12},{8,0},{12,4},{16,24},{20,28},{24,16},{28,20},{32,40},... | collective-permute-start | bytes 1769480 | tf_op jit(solution)/shard_map/ppermute | solution.py:34
  228.1 9.6 %all-to-all-start.2 = ((bf16[4,24,1536]{2,1,0:T(8,128)(2,1)}), bf16[4,24,1536]{2,1,0:T(8,128)(2,1)S(1)}, u32[]{:S(2)}, u32[]{:S(2)}) async-start(bf16[4,24,1536]{2,1,0:T(8,128)(2,1)} %broadcast_in_dim.46), calls=%async_computation.5 | async-start | bytes 589824 | tf_op jit(solution)/shard_map/all_to_all | solution.py:26
  237.7 5.7 collective-permute-start.4
  241.4 41.4 %copy-start.3 = (bf16[384,1536]{1,0:T(8,128)(2,1)}, bf16[384,1536]{1,0:T(8,128)(2,1)S(1)}, u32[]{:S(2)}) copy-start(bf16[384,1536]{1,0:T(8,128)(2,1)S(1)} %maximum_select_fusion.5) | copy-start | bytes 3538948
  241.4 79.0 %collective-permute-start.2 = (bf16[384,1536]{1,0:T(8,128)(2,1)S(1)}, bf16[384,1536]{1,0:T(8,128)(2,1)}, u32[]{:S(2)}, u32[]{:S(2)}) collective-permute-start(bf16[384,1536]{1,0:T(8,128)(2,1)S(1)} %maximum_select_fusion.5), channel_id=1, source_target_pairs={{0,16},{4,20},{8,24},{12,28},{16,0},{20,4},{24,8},{28,12},{32,48},... | collective-permute-start | bytes 3538952 | tf_op jit(solution)/shard_map/ppermute | solution.py:34
  243.6 37.0 %collective-permute-start.5 = (bf16[192,1536]{1,0:T(8,128)(2,1)S(1)}, bf16[192,1536]{1,0:T(8,128)(2,1)S(1)}, u32[]{:S(2)}, u32[]{:S(2)}) collective-permute-start(bf16[192,1536]{1,0:T(8,128)(2,1)S(1)} %maximum_select_fusion.8), channel_id=1, source_target_pairs={{0,8},{4,12},{8,0},{12,4},{16,24},{20,28},{24,16},{28,20},{32,40},... | collective-permute-start | bytes 1769480 | tf_op jit(solution)/shard_map/ppermute | solution.py:34
  281.0 115.9 %collective-permute-start.6 = (bf16[384,1536]{1,0:T(8,128)(2,1)S(1)}, bf16[384,1536]{1,0:T(8,128)(2,1)S(1)}, u32[]{:S(2)}, u32[]{:S(2)}) collective-permute-start(bf16[384,1536]{1,0:T(8,128)(2,1)S(1)} %maximum_select_fusion.6), channel_id=1, source_target_pairs={{0,16},{4,20},{8,24},{12,28},{16,0},{20,4},{24,8},{28,12},{32,48},... | collective-permute-start | bytes 3538952 | tf_op jit(solution)/shard_map/ppermute | solution.py:34
  323.1 78.6 %copy-start.6 = (f32[24,1536]{1,0:T(8,128)S(1)}, f32[24,1536]{1,0:T(8,128)}, u32[]{:S(2)}) copy-start(f32[24,1536]{1,0:T(8,128)} %param.17) | copy-start | bytes 442372
  323.1 78.6 %copy-start.7 = (f32[24,1536]{1,0:T(8,128)S(1)}, f32[24,1536]{1,0:T(8,128)}, u32[]{:S(2)}) copy-start(f32[24,1536]{1,0:T(8,128)} %param.16) | copy-start | bytes 442372
  323.2 80.8 %collective-permute-start.3 = (bf16[768,1536]{1,0:T(8,128)(2,1)S(1)}, bf16[768,1536]{1,0:T(8,128)(2,1)}, u32[]{:S(2)}, u32[]{:S(2)}) collective-permute-start(bf16[768,1536]{1,0:T(8,128)(2,1)S(1)} %maximum_select_fusion.3), channel_id=1, source_target_pairs={{0,32},{4,36},{8,40},{12,44},{16,48},{20,52},{24,56},{28,60},{32,0... | collective-permute-start | bytes 7077896 | tf_op jit(solution)/shard_map/ppermute | solution.py:34
  398.7 154.4 %collective-permute-start.7 = (bf16[768,1536]{1,0:T(8,128)(2,1)}, bf16[768,1536]{1,0:T(8,128)(2,1)}, u32[]{:S(2)}, u32[]{:S(2)}) collective-permute-start(bf16[768,1536]{1,0:T(8,128)(2,1)} %maximum_select_fusion.4), channel_id=1, source_target_pairs={{0,32},{4,36},{8,40},{12,44},{16,48},{20,52},{24,56},{28,60},{32,0... | collective-permute-start | bytes 7077896 | tf_op jit(solution)/shard_map/ppermute | solution.py:34
  407.7 2.2 copy-start.2
  607.1 8.8 %copy-start.8 = (s32[4]{0:T(128)S(1)}, s32[4]{0:T(128)}, u32[]{:S(2)}) copy-start(s32[4]{0:T(128)} %param.12) | copy-start | bytes 52
  607.1 8.8 %copy-start.5 = (f32[24,2,1536]{2,1,0:T(2,128)S(1)}, f32[24,2,1536]{2,1,0:T(2,128)}, u32[]{:S(2)}) copy-start(f32[24,2,1536]{2,1,0:T(2,128)} %param.14) | copy-start | bytes 884740
  607.1 115.9 %all-to-all-start.4 = ((bf16[64,96,384]{2,1,0:T(8,128)(2,1)}), bf16[64,96,384]{2,1,0:T(8,128)(2,1)}, u32[]{:S(2)}, u32[]{:S(2)}) async-start(bf16[64,96,384]{2,1,0:T(8,128)(2,1)} %stack.14), calls=%async_computation.7 | async-start | bytes 9437184 | tf_op jit(solution)/shard_map/all_to_all | solution.py:161
  723.1 11.0 %copy-start.1 = (bf16[1024,4,384]{2,1,0:T(4,128)(2,1)S(1)}, bf16[1024,4,384]{2,1,0:T(4,128)(2,1)}, u32[]{:S(2)}) copy-start(bf16[1024,4,384]{2,1,0:T(4,128)(2,1)} %param.11) | copy-start | bytes 9437188
Sparse Core Ops, SparseCore 0:
  78.6 27.4 reduce-scatter.3
  108.7 54.4 reduce-scatter.5
  165.7 34.4 reduce-scatter.7
